TPU v7x, 32 devices: a whole 2x2x4 slice. The times are simulated.
32 devices in a mesh: outer: 4 (over y, x), inner: 8 (over z, core).
Axes of the slice: x: 2, y: 2, z: 4, core: 2. Of those that a mesh axis runs over, the one named last changes fastest.
Arguments:
- queries: bfloat16 [8192, 1024], P(('outer', 'inner')), may hold values from -480 to 480
- keys: bfloat16 [8192, 512], P(('outer', 'inner')), may hold values from -8 to 8
- values: bfloat16 [8192, 512], P(('outer', 'inner')), may hold values from -4 to 4
- residual: bfloat16 [8192, 1024], P(('outer', 'inner')), may hold values from -5 to 5
- norm_gain: float32 [1024], replicated, may hold values from 0.1 to 1.9
- w_gate: bfloat16 [8, 1024, 512], P('inner'), may hold values from -0.1875 to 0.1875
- w_up: bfloat16 [8, 1024, 512], P('inner'), may hold values from -0.1875 to 0.1875
- w_down: bfloat16 [8, 512, 1024], P('inner'), may hold values from -0.25 to 0.25
- routes: int32 [8192, 2], P(('outer', 'inner')), may hold values from 0 to 7, all different within a row; in each aligned block of 256 rows (0 to 255, 256 to 511, ...) at most 128 rows name the same one
- gates: float32 [8192, 2], P(('outer', 'inner')), may hold values from 0.2 to 1
Outputs:
- layer_out: bfloat16 [8192, 1024], P(('outer', 'inner'))
Inputs may be any that keep to these rules, and one draw needn't show every extreme that they name: `routes`: A patch's two experts differ. Within one block of 256 patches no expert is picked more than 128 times, and in some block one expert is picked exactly 128 times.
All inputs are finite; a program needn't handle non-finite values.
Results may differ from a plain program's by a relative error of at most 0.0085.
Values may be sent and summed in bfloat16 or wider, within the bound.
A program may use at most 64 MiB of HBM per device.

v0:
```python
import math
import jax
import jax.numpy as jnp
from jax import lax
from jax.sharding import PartitionSpec as P

D = 1024
QH = 8
KVH = 4
DH = 128
BACK = 3


def shifted(value, axis, steps):
    count = lax.axis_size(axis)
    first, last = (max(0, -steps), min(count, count - steps))
    return lax.ppermute(value, axis, [(source, source + steps) for source in range(first, last)])


def feed_forward(rows, gate_matrix, up_matrix, down_matrix):
    gate_part = jnp.dot(rows, gate_matrix, preferred_element_type=jnp.float32)
    up_part = jnp.dot(rows, up_matrix, preferred_element_type=jnp.float32)
    inner_act = (jax.nn.silu(gate_part) * up_part).astype(jnp.bfloat16)
    return jnp.dot(inner_act, down_matrix, preferred_element_type=jnp.float32).astype(jnp.bfloat16)


def local(queries, keys, values, residual, norm_gain, w_gate, w_up, w_down, routes, gates):
    tok_rows = queries.shape[0]
    groups = QH // KVH
    device_index = lax.axis_index(("outer", "inner"))
    current = (keys, values)
    earlier = []
    for step_index in range(BACK):
        current = shifted((current[0], current[1]), ("outer", "inner"), 1)
        earlier = [current] + earlier
    key_window = jnp.concatenate([block_pair[0] for block_pair in earlier] + [keys], 0)
    value_window = jnp.concatenate([block_pair[1] for block_pair in earlier] + [values], 0)
    window_rows = key_window.shape[0]
    query_heads = queries.reshape(tok_rows, KVH, groups, DH)
    key_heads = key_window.reshape(window_rows, KVH, DH)
    value_heads = value_window.reshape(window_rows, KVH, DH)
    scores = jnp.einsum(
        "tkgd,skd->kgts", query_heads, key_heads, preferred_element_type=jnp.float32
    ) * (1.0 / math.sqrt(DH))
    query_pos = device_index * tok_rows + jnp.arange(tok_rows, dtype=jnp.int32)
    key_pos = (device_index - BACK) * tok_rows + jnp.arange(window_rows, dtype=jnp.int32)
    allowed = (key_pos[None, :] >= 0) & (key_pos[None, :] <= query_pos[:, None])
    scores = jnp.where(allowed, scores, -jnp.inf)
    highest = jnp.max(scores, -1, keepdims=True)
    expd = jnp.exp(scores - highest)
    weights = (expd / jnp.sum(expd, -1, keepdims=True)).astype(jnp.bfloat16)
    mixed = jnp.einsum("kgts,skd->tkgd", weights, value_heads, preferred_element_type=jnp.float32)
    attended = mixed.astype(jnp.bfloat16).reshape(tok_rows, QH * DH)
    stream = residual.astype(jnp.float32) + attended.astype(jnp.float32)
    mean_sq = jnp.mean(stream * stream, -1, keepdims=True)
    normed = (stream * lax.rsqrt(mean_sq + 1e-06) * norm_gain).astype(jnp.bfloat16)
    owners = lax.axis_size("inner")
    capacity = 4 * tok_rows // owners
    picks = routes.reshape(-1)
    one_hot = (picks[:, None] == jnp.arange(owners, dtype=jnp.int32)[None, :]).astype(jnp.int32)
    order_rank = jnp.sum((jnp.cumsum(one_hot, 0) - 1) * one_hot, 1)
    slot_index = picks * capacity + order_rank
    slot_pair = slot_index.reshape(tok_rows, 2)
    slot_grid = jnp.arange(owners * capacity, dtype=jnp.int32)[:, None]
    placing = ((slot_pair[None, :, 0] == slot_grid) | (slot_pair[None, :, 1] == slot_grid)).astype(
        jnp.bfloat16
    )
    outgoing = (
        jnp.dot(placing, normed, preferred_element_type=jnp.float32)
        .astype(jnp.bfloat16)
        .reshape(owners, capacity, D)
    )
    gate_matrix = w_gate[0]
    up_matrix = w_up[0]
    down_matrix = w_down[0]
    arrived = lax.all_to_all(outgoing, "inner", split_axis=0, concat_axis=0, tiled=True)
    results = feed_forward(arrived.reshape(-1, D), gate_matrix, up_matrix, down_matrix).reshape(
        arrived.shape
    )
    returned = lax.all_to_all(results, "inner", split_axis=0, concat_axis=0, tiled=True)
    picked = (
        returned.reshape(owners * capacity, D)[slot_index]
        .astype(jnp.float32)
        .reshape(tok_rows, 2, D)
    )
    mixture = jnp.sum(gates[:, :, None] * picked, 1)
    return (stream + mixture).astype(jnp.bfloat16)


def solution(mesh):
    return jax.shard_map(
        local,
        mesh=mesh,
        in_specs=(
            P(("outer", "inner"), None),
            P(("outer", "inner"), None),
            P(("outer", "inner"), None),
            P(("outer", "inner"), None),
            P(),
            P("inner", None, None),
            P("inner", None, None),
            P("inner", None, None),
            P(("outer", "inner"), None),
            P(("outer", "inner"), None),
        ),
        out_specs=P(("outer", "inner"), None),
        check_vma=False,
    )
```

profile of v0, /device:TPU:4, one launch (start us, length us, event | category | flops | bytes accessed | tf_op | source)
XLA Modules:
  0.0 177.8 jit_solution(39388173408413153)
XLA Ops:
  0.0 0.0 copy-start
  0.0 1.2 copy.28
  1.2 1.9 %collective-permute-start.3 = (bf16[256,512]{0,1:T(8,128)(2,1)S(1)}, bf16[256,512]{0,1:T(8,128)(2,1)S(1)}, u32[]{:S(2)}, u32[]{:S(2)}) collective-permute-start(bf16[256,512]{0,1:T(8,128)(2,1)S(1)} %copy.28), channel_id=1, source_target_pairs={{0,1},{1,2},{2,3},{3,4},{4,5},{5,6},{6,7},{7,8},{8,9},{9,10},{10,1... | collective-permute-start | bytes 786440 | tf_op jit(solution)/shard_map/ppermute | solution.py:17
  3.1 3.6 %collective-permute-start = (bf16[256,512]{1,0:T(8,128)(2,1)}, bf16[256,512]{1,0:T(8,128)(2,1)S(1)}, u32[]{:S(2)}, u32[]{:S(2)}) collective-permute-start(bf16[256,512]{1,0:T(8,128)(2,1)} %param.12), channel_id=1, source_target_pairs={{0,1},{1,2},{2,3},{3,4},{4,5},{5,6},{6,7},{7,8},{8,9},{9,10},{10,1... | collective-permute-start | bytes 786440 | tf_op jit(solution)/shard_map/ppermute | solution.py:17
  6.7 0.8 copy.35
  7.6 0.1 eq.59
  7.7 1.1 reduce-window.6
  8.9 0.2 slice_reduce_fusion.2
  9.1 0.1 eq.55
  9.3 0.1 fusion.29
  9.4 3.1 %collective-permute-done.3 = bf16[256,512]{0,1:T(8,128)(2,1)S(1)} collective-permute-done((bf16[256,512]{0,1:T(8,128)(2,1)S(1)}, bf16[256,512]{0,1:T(8,128)(2,1)S(1)}, u32[]{:S(2)}, u32[]{:S(2)}) %collective-permute-start.3) | collective-permute-done | bytes 262176 | tf_op jit(solution)/shard_map/ppermute | solution.py:17
  12.5 1.9 %collective-permute-start.4 = (bf16[256,512]{0,1:T(8,128)(2,1)S(1)}, bf16[256,512]{0,1:T(8,128)(2,1)}, u32[]{:S(2)}, u32[]{:S(2)}) collective-permute-start(bf16[256,512]{0,1:T(8,128)(2,1)S(1)} %collective-permute-done.3), channel_id=1, source_target_pairs={{0,1},{1,2},{2,3},{3,4},{4,5},{5,6},{6,7},{7,8},{8,9},{9,10},{10,1... | collective-permute-start | bytes 786440 | tf_op jit(solution)/shard_map/ppermute | solution.py:17
  14.4 0.9 collective-permute-done
  15.3 1.9 %collective-permute-start.1 = (bf16[256,512]{1,0:T(8,128)(2,1)S(1)}, bf16[256,512]{1,0:T(8,128)(2,1)S(1)}, u32[]{:S(2)}, u32[]{:S(2)}) collective-permute-start(bf16[256,512]{1,0:T(8,128)(2,1)S(1)} %collective-permute-done), channel_id=1, source_target_pairs={{0,1},{1,2},{2,3},{3,4},{4,5},{5,6},{6,7},{7,8},{8,9},{9,10},{10,1... | collective-permute-start | bytes 786440 | tf_op jit(solution)/shard_map/ppermute | solution.py:17
  17.2 0.1 reduce_sum.42
  17.4 6.5 %collective-permute-done.4 = bf16[256,512]{0,1:T(8,128)(2,1)} collective-permute-done((bf16[256,512]{0,1:T(8,128)(2,1)S(1)}, bf16[256,512]{0,1:T(8,128)(2,1)}, u32[]{:S(2)}, u32[]{:S(2)}) %collective-permute-start.4) | collective-permute-done | bytes 262176 | tf_op jit(solution)/shard_map/ppermute | solution.py:17
  23.9 1.9 %collective-permute-start.5 = (bf16[256,512]{0,1:T(8,128)(2,1)}, bf16[256,512]{0,1:T(8,128)(2,1)}, u32[]{:S(2)}, u32[]{:S(2)}) collective-permute-start(bf16[256,512]{0,1:T(8,128)(2,1)} %collective-permute-done.4), channel_id=1, source_target_pairs={{0,1},{1,2},{2,3},{3,4},{4,5},{5,6},{6,7},{7,8},{8,9},{9,10},{10,1... | collective-permute-start | bytes 786440 | tf_op jit(solution)/shard_map/ppermute | solution.py:17
  25.8 0.8 collective-permute-done.1
  26.6 1.9 %collective-permute-start.2 = (bf16[256,512]{1,0:T(8,128)(2,1)S(1)}, bf16[256,512]{1,0:T(8,128)(2,1)}, u32[]{:S(2)}, u32[]{:S(2)}) collective-permute-start(bf16[256,512]{1,0:T(8,128)(2,1)S(1)} %collective-permute-done.1), channel_id=1, source_target_pairs={{0,1},{1,2},{2,3},{3,4},{4,5},{5,6},{6,7},{7,8},{8,9},{9,10},{10,1... | collective-permute-start | bytes 786440 | tf_op jit(solution)/shard_map/ppermute | solution.py:17
  28.5 1.1 compare_and_fusion
  29.6 0.0 copy-done.5
  29.6 1.2 reshape.106
  30.7 0.2 slice_reduce_fusion.1
  30.9 7.3 %collective-permute-done.2 = bf16[256,512]{1,0:T(8,128)(2,1)} collective-permute-done((bf16[256,512]{1,0:T(8,128)(2,1)S(1)}, bf16[256,512]{1,0:T(8,128)(2,1)}, u32[]{:S(2)}, u32[]{:S(2)}) %collective-permute-start.2) | collective-permute-done | bytes 262176 | tf_op jit(solution)/shard_map/ppermute | solution.py:17
  38.3 1.3 pad_maximum_fusion
  39.5 0.5 copy.27
  40.1 0.0 collective-permute-done.5
  40.1 1.2 pad_maximum_fusion.1
  41.3 7.1 %fusion.35 = (f32[4,2,256]{2,1,0:T(2,128)S(1)}, f32[4,2,256,1024]{2,3,1,0:T(8,128)}) fusion(pred[256,1024]{0,1:T(8,128)(4,1)} %compare_and_fusion, bf16[1024,4,128,1]{0,2,3,1:T(8,128)(2,1)S(1)} %bitcast.57, bf16[256,4,2,128]{3,2,1,0:T(2,128)(2,1)} %reshape.106), kind=kOutput, calls=%fused_computation.58 | convolution fusion | flops 545260544 | bytes 10231808 | tf_op jit(solution)/shard_map/sub | solution.py:50
  48.5 5.2 %fusion.7 = f32[4,128,2,256]{3,1,2,0:T(8,128)} fusion(bf16[1024,4,128,1]{0,2,3,1:T(8,128)(2,1)S(1)} %bitcast.56, f32[4,2,256,1024]{2,3,1,0:T(8,128)} %get-tuple-element.10, f32[4,2,256]{2,1,0:T(2,128)S(1)} %get-tuple-element.9), kind=kOutput, calls=%fused_computation.15 | convolution fusion | flops 541589504 | bytes 10493952 | tf_op jit(solution)/shard_map/kgts,skd->tkgd/dot_general | solution.py:52
  53.6 1.6 copy.33
  55.3 0.2 multiply_reduce_fusion.1
  55.5 0.8 convolution_convert_fusion.1
  56.4 0.0 copy-done.1
  56.4 0.0 copy-start.11
  56.4 51.6 %all_to_all.10 = bf16[8,128,1024]{2,1,0:T(8,128)(2,1)S(1)} all-to-all(bf16[8,128,1024]{2,1,0:T(8,128)(2,1)S(1)} %bitcast.52), channel_id=1, replica_groups=mesh['outer'=4,'inner'=8] {'inner'}, dimensions={0} | all-to-all | bytes 4194304 | tf_op jit(solution)/shard_map/all_to_all | solution.py:76
  108.0 2.6 %fusion.11 = f32[1024,512]{1,0:T(8,128)} fusion(bf16[1024,1024]{1,0:T(8,128)(2,1)S(1)} %bitcast.54, bf16[1,1024,512]{2,1,0:T(8,128)(2,1)S(1)} %copy-done.11), kind=kOutput, calls=%fused_computation.20 | convolution fusion | flops 1073741824 | bytes 5242880 | tf_op jit(solution)/shard_map/dot_general | solution.py:21
  110.6 5.6 %convolution_convert_fusion = bf16[1024,1024]{1,0:T(8,128)(2,1)} fusion(f32[1024,512]{1,0:T(8,128)} %fusion.11, bf16[1024,1024]{1,0:T(8,128)(2,1)S(1)} %bitcast.55, bf16[1,512,1024]{2,1,0:T(8,128)(2,1)S(1)} %copy-done, bf16[1,1024,512]{2,1,0:T(8,128)(2,1)} %param.16), kind=kOutput, calls=%fused_computation.12 | convolution fusion | flops 2151677952 | bytes 8388608 | tf_op jit(solution)/shard_map/dot_general | solution.py:24
  116.2 3.9 %all-to-all-start.1 = ((bf16[8,128,1024]{2,1,0:T(8,128)(2,1)}), bf16[8,128,1024]{2,1,0:T(8,128)(2,1)S(1)}, u32[]{:S(2)}, u32[]{:S(2)}) async-start(bf16[8,128,1024]{2,1,0:T(8,128)(2,1)} %bitcast.53), calls=%async_computation.1 | async-start | bytes 4194304 | tf_op jit(solution)/shard_map/all_to_all | solution.py:80
  120.1 0.1 mul.89
  120.3 0.1 copy.34
  120.5 48.5 %all-to-all-done.1 = bf16[8,128,1024]{2,1,0:T(8,128)(2,1)S(1)} async-done(((bf16[8,128,1024]{2,1,0:T(8,128)(2,1)}), bf16[8,128,1024]{2,1,0:T(8,128)(2,1)S(1)}, u32[]{:S(2)}, u32[]{:S(2)}) %all-to-all-start.1) | async-done | bytes 2097184 | tf_op jit(solution)/shard_map/all_to_all | solution.py:80
  168.9 2.8 %gather_fusion = bf16[512,1024]{1,0:T(8,128)(2,1)} fusion(bf16[1024,1024]{1,0:T(8,128)(2,1)S(1)} %bitcast.51, s32[1024]{0:T(1024)S(1)} %pad_clamp_fusion), kind=kCustom, calls=%fused_computation | custom fusion | bytes 2099200 | tf_op jit(solution)/shard_map/gather | solution.py:82
  171.7 2.4 %reshape.113 = f32[256,2,1024]{2,1,0:T(2,128)S(1)} reshape(bf16[512,1024]{1,0:T(8,128)(2,1)} %gather_fusion) | data formatting | bytes 3145728 | tf_op jit(solution)/shard_map/convert_element_type | solution.py:83
  174.1 0.0 copy-start.2
  174.1 0.0 copy-start.4
  174.1 2.6 %multiply_reduce_fusion = f32[256,1024]{1,0:T(8,128)S(1)} fusion(f32[256,2,1024]{2,1,0:T(2,128)S(1)} %reshape.113, f32[256,2]{1,0:T(8,128)S(1)} %copy.34), kind=kLoop, calls=%fused_computation.10 | loop fusion | flops 786432 | bytes 3147776 | tf_op jit(solution)/shard_map/reduce_sum | solution.py:86
  176.8 1.1 add_convert_fusion
  (28 shorter events, 0.1 us)
Async XLA Ops:
  0.0 110.6 %copy-start = (bf16[1,512,1024]{2,1,0:T(8,128)(2,1)S(1)}, bf16[1,512,1024]{2,1,0:T(8,128)(2,1)}, u32[]{:S(2)}) copy-start(bf16[1,512,1024]{2,1,0:T(8,128)(2,1)} %param.17) | copy-start | bytes 3145732
  0.0 29.6 %copy-start.5 = (bf16[256,1024]{1,0:T(8,128)(2,1)S(1)}, bf16[256,1024]{1,0:T(8,128)(2,1)}, u32[]{:S(2)}) copy-start(bf16[256,1024]{1,0:T(8,128)(2,1)} %param.10) | copy-start | bytes 1572868
  1.2 11.3 %collective-permute-start.3 = (bf16[256,512]{0,1:T(8,128)(2,1)S(1)}, bf16[256,512]{0,1:T(8,128)(2,1)S(1)}, u32[]{:S(2)}, u32[]{:S(2)}) collective-permute-start(bf16[256,512]{0,1:T(8,128)(2,1)S(1)} %copy.28), channel_id=1, source_target_pairs={{0,1},{1,2},{2,3},{3,4},{4,5},{5,6},{6,7},{7,8},{8,9},{9,10},{10,1... | collective-permute-start | bytes 786440 | tf_op jit(solution)/shard_map/ppermute | solution.py:17
  3.1 12.2 %collective-permute-start = (bf16[256,512]{1,0:T(8,128)(2,1)}, bf16[256,512]{1,0:T(8,128)(2,1)S(1)}, u32[]{:S(2)}, u32[]{:S(2)}) collective-permute-start(bf16[256,512]{1,0:T(8,128)(2,1)} %param.12), channel_id=1, source_target_pairs={{0,1},{1,2},{2,3},{3,4},{4,5},{5,6},{6,7},{7,8},{8,9},{9,10},{10,1... | collective-permute-start | bytes 786440 | tf_op jit(solution)/shard_map/ppermute | solution.py:17
  12.5 18.4 %copy-start.6 = (bf16[256,512]{0,1:T(8,128)(2,1)}, bf16[256,512]{0,1:T(8,128)(2,1)S(1)}, u32[]{:S(2)}) copy-start(bf16[256,512]{0,1:T(8,128)(2,1)S(1)} %collective-permute-done.3) | copy-start | bytes 786436
  12.5 11.4 %collective-permute-start.4 = (bf16[256,512]{0,1:T(8,128)(2,1)S(1)}, bf16[256,512]{0,1:T(8,128)(2,1)}, u32[]{:S(2)}, u32[]{:S(2)}) collective-permute-start(bf16[256,512]{0,1:T(8,128)(2,1)S(1)} %collective-permute-done.3), channel_id=1, source_target_pairs={{0,1},{1,2},{2,3},{3,4},{4,5},{5,6},{6,7},{7,8},{8,9},{9,10},{10,1... | collective-permute-start | bytes 786440 | tf_op jit(solution)/shard_map/ppermute | solution.py:17
  15.3 15.6 %copy-start.7 = (bf16[256,512]{1,0:T(8,128)(2,1)}, bf16[256,512]{1,0:T(8,128)(2,1)S(1)}, u32[]{:S(2)}) copy-start(bf16[256,512]{1,0:T(8,128)(2,1)S(1)} %collective-permute-done) | copy-start | bytes 786436
  15.3 11.3 %collective-permute-start.1 = (bf16[256,512]{1,0:T(8,128)(2,1)S(1)}, bf16[256,512]{1,0:T(8,128)(2,1)S(1)}, u32[]{:S(2)}, u32[]{:S(2)}) collective-permute-start(bf16[256,512]{1,0:T(8,128)(2,1)S(1)} %collective-permute-done), channel_id=1, source_target_pairs={{0,1},{1,2},{2,3},{3,4},{4,5},{5,6},{6,7},{7,8},{8,9},{9,10},{10,1... | collective-permute-start | bytes 786440 | tf_op jit(solution)/shard_map/ppermute | solution.py:17
  23.9 16.2 %collective-permute-start.5 = (bf16[256,512]{0,1:T(8,128)(2,1)}, bf16[256,512]{0,1:T(8,128)(2,1)}, u32[]{:S(2)}, u32[]{:S(2)}) collective-permute-start(bf16[256,512]{0,1:T(8,128)(2,1)} %collective-permute-done.4), channel_id=1, source_target_pairs={{0,1},{1,2},{2,3},{3,4},{4,5},{5,6},{6,7},{7,8},{8,9},{9,10},{10,1... | collective-permute-start | bytes 786440 | tf_op jit(solution)/shard_map/ppermute | solution.py:17
  26.6 4.4 %copy-start.8 = (bf16[256,512]{1,0:T(8,128)(2,1)}, bf16[256,512]{1,0:T(8,128)(2,1)S(1)}, u32[]{:S(2)}) copy-start(bf16[256,512]{1,0:T(8,128)(2,1)S(1)} %collective-permute-done.1) | copy-start | bytes 786436
  26.6 11.7 %collective-permute-start.2 = (bf16[256,512]{1,0:T(8,128)(2,1)S(1)}, bf16[256,512]{1,0:T(8,128)(2,1)}, u32[]{:S(2)}, u32[]{:S(2)}) collective-permute-start(bf16[256,512]{1,0:T(8,128)(2,1)S(1)} %collective-permute-done.1), channel_id=1, source_target_pairs={{0,1},{1,2},{2,3},{3,4},{4,5},{5,6},{6,7},{7,8},{8,9},{9,10},{10,1... | collective-permute-start | bytes 786440 | tf_op jit(solution)/shard_map/ppermute | solution.py:17
  53.6 1.6 copy-start.3
  53.6 1.9 %copy-start.9 = (f32[1024]{0:T(1024)S(1)}, f32[1024]{0:T(1024)}, u32[]{:S(2)}) copy-start(f32[1024]{0:T(1024)} %param.14) | copy-start | bytes 12292
  55.3 1.1 copy-start.1
  56.4 51.6 %copy-start.11 = (bf16[1,1024,512]{2,1,0:T(8,128)(2,1)S(1)}, bf16[1,1024,512]{2,1,0:T(8,128)(2,1)}, u32[]{:S(2)}) copy-start(bf16[1,1024,512]{2,1,0:T(8,128)(2,1)} %param.15) | copy-start | bytes 3145732
  116.2 4.1 %copy-start.10 = (f32[256,2]{0,1:T(2,128)S(1)}, f32[256,2]{0,1:T(2,128)}, u32[]{:S(2)}) copy-start(f32[256,2]{0,1:T(2,128)} %param.19) | copy-start | bytes 6148
  116.2 52.7 %all-to-all-start.1 = ((bf16[8,128,1024]{2,1,0:T(8,128)(2,1)}), bf16[8,128,1024]{2,1,0:T(8,128)(2,1)S(1)}, u32[]{:S(2)}, u32[]{:S(2)}) async-start(bf16[8,128,1024]{2,1,0:T(8,128)(2,1)} %bitcast.53), calls=%async_computation.1 | async-start | bytes 4194304 | tf_op jit(solution)/shard_map/all_to_all | solution.py:80
  174.1 2.7 %copy-start.2 = (f32[256,1024]{1,0:T(8,128)S(1)}, f32[256,1024]{1,0:T(8,128)}, u32[]{:S(2)}) copy-start(f32[256,1024]{1,0:T(8,128)} %copy-done.1) | copy-start | bytes 3145732
  174.1 2.7 %copy-start.4 = (bf16[256,1024]{1,0:T(8,128)(2,1)S(1)}, bf16[256,1024]{1,0:T(8,128)(2,1)}, u32[]{:S(2)}) copy-start(bf16[256,1024]{1,0:T(8,128)(2,1)} %param.13) | copy-start | bytes 1572868
where the time goes:
time: 178 us
  waiting for transfers between devices  67.1 us (38%)
  blocking collectives  51.6 us (29%)
  matrix products  21.4 us (12%)
  starting transfers between devices  17.1 us (10%)
  local copies, waits for them, and re-layouts  11.6 us (7%)
  other arithmetic  8.8 us (5%)
    all_to_all x1, blocking collectives, local(): lax.all_to_all(outgoing, 'inner', split_axis=0, concat_axis=0, tiled=True)  51.6 us
    all_to_all x1, waiting for transfers between devices, local(): lax.all_to_all(results, 'inner', split_axis=0, concat_axis=0, tiled=True)  48.5 us
    ppermute x6, waiting for transfers between devices, shifted(): lax.ppermute(value, axis, [(source, source + steps) for source in range(f...  18.6 us
    ppermute x6, starting transfers between devices, shifted(): lax.ppermute(value, axis, [(source, source + steps) for source in range(f...  13.1 us
    sub x1, matrix products, local(): expd = jnp.exp(scores - highest)  7.12 us
    dot_general x1, matrix products, feed_forward(): jnp.dot(inner_act, down_matrix, preferred_element_type=jnp.float32)  5.63 us
    dot_general x1, matrix products, local(): jnp.einsum('kgts,skd->tkgd', weights, value_heads, preferred_element_type...  5.18 us
    all_to_all x1, starting transfers between devices, local(): lax.all_to_all(results, 'inner', split_axis=0, concat_axis=0, tiled=True)  3.91 us
  transfers between devices with their start and end apart: 7, of which 6 were waited for; matrix products, arithmetic and copies ran while one was open for 4% of the time, Pallas kernels for 0%

commit v1 on v0

--- a/solution.py
+++ b/solution.py
@@ -1,14 +1,39 @@
+import functools
 import math
 import jax
 import jax.numpy as jnp
 from jax import lax
 from jax.sharding import PartitionSpec as P
+from jax.lax import axis_index, axis_size, ppermute
 
 D = 1024
 QH = 8
 KVH = 4
 DH = 128
 BACK = 3
+
+
+def press_skins(mine_x, ndim_at, which_dim):
+    top, y2 = (axis_size("inner"), axis_index("inner"))
+    carry_in = mine_x.shape[ndim_at] // top
+    known = list(mine_x.shape)
+    known[ndim_at] = carry_in
+    next_value = known[which_dim]
+    known[which_dim] = next_value * top
+    finding = jnp.zeros(known, mine_x.dtype)
+    for src_i in tuple(range(top)):
+        a_now = lax.dynamic_slice_in_dim(mine_x, (y2 ^ src_i) * carry_in, carry_in, axis=ndim_at)
+        if src_i:
+            a_now = ppermute(
+                a_now, axis_name="inner", perm=[(num, num ^ src_i) for num in range(top)]
+            )
+        finding = lax.dynamic_update_slice_in_dim(
+            finding, a_now, (y2 ^ src_i) * next_value, axis=which_dim
+        )
+    return finding
+
+
+write_zone = functools.partial(press_skins, ndim_at=0, which_dim=0)
 
 
 def shifted(value, axis, steps):
@@ -73,7 +98,7 @@
     gate_matrix = w_gate[0]
     up_matrix = w_up[0]
     down_matrix = w_down[0]
-    arrived = lax.all_to_all(outgoing, "inner", split_axis=0, concat_axis=0, tiled=True)
+    arrived = write_zone(outgoing)
     results = feed_forward(arrived.reshape(-1, D), gate_matrix, up_matrix, down_matrix).reshape(
         arrived.shape
     )

time: 178 us -> 176 us (0.989)
  blocking collectives: 51.6 us -> 0 us
  waiting for transfers between devices: 67.1 us -> 101 us
  starting transfers between devices: 17.1 us -> 30.9 us
    all_to_all x1 -> x0, blocking collectives: 51.6 us -> none  [local(): lax.all_to_all(outgoing, 'inner', split_axis=0, concat_axis=0, tiled=True)]
    ppermute x0 -> x7, waiting for transfers between devices: none -> 34.2 us  [press_skins(): ppermute(a_now, axis_name='inner', perm=[(num, num ^ src_i) for num in ra...]
    all_to_all x1, starting transfers between devices: 3.91 us -> 13.2 us  [local(): lax.all_to_all(results, 'inner', split_axis=0, concat_axis=0, tiled=True)]
    ppermute x0 -> x7, starting transfers between devices: none -> 4.56 us  [press_skins(): ppermute(a_now, axis_name='inner', perm=[(num, num ^ src_i) for num in ra...]
  transfers between devices with their start and end apart: 7 -> 14, of which waited for: 6 -> 10; matrix products, arithmetic and copies ran while one was open for 4% -> 4% of each run, Pallas kernels for 0% -> 0%
where the time goes in v1:
time: 176 us; the launch traced here: 175 us
  waiting for transfers between devices  101 us (57%)
  starting transfers between devices  30.9 us (18%)
  matrix products  21.3 us (12%)
  local copies, waits for them, and re-layouts  12.3 us (7%)
  other arithmetic  8.73 us (5%)
    all_to_all x1, waiting for transfers between devices, local(): lax.all_to_all(results, 'inner', split_axis=0, concat_axis=0, tiled=True)  48.7 us
    ppermute x7, waiting for transfers between devices, press_skins(): ppermute(a_now, axis_name='inner', perm=[(num, num ^ src_i) for num in ra...  34.2 us
    ppermute x6, waiting for transfers between devices, shifted(): lax.ppermute(value, axis, [(source, source + steps) for source in range(f...  18.5 us
    all_to_all x1, starting transfers between devices, local(): lax.all_to_all(results, 'inner', split_axis=0, concat_axis=0, tiled=True)  13.2 us
    ppermute x6, starting transfers between devices, shifted(): lax.ppermute(value, axis, [(source, source + steps) for source in range(f...  13.1 us
    sub x1, matrix products, local(): expd = jnp.exp(scores - highest)  7.11 us
    dot_general x1, matrix products, feed_forward(): jnp.dot(inner_act, down_matrix, preferred_element_type=jnp.float32)  5.63 us
    dot_general x1, matrix products, local(): jnp.einsum('kgts,skd->tkgd', weights, value_heads, preferred_element_type...  5.15 us
  transfers between devices with their start and end apart: 14, of which 10 were waited for; matrix products, arithmetic and copies ran while one was open for 4% of the time, Pallas kernels for 0%

profile of v1, /device:TPU:4, one launch (start us, length us, event | category | flops | bytes accessed | tf_op | source)
XLA Modules:
  0.0 175.0 jit_solution(8013081185423981744)
XLA Ops:
  0.0 1.2 copy.28
  1.2 1.9 %collective-permute-start.3 = (bf16[256,512]{0,1:T(8,128)(2,1)S(1)}, bf16[256,512]{0,1:T(8,128)(2,1)S(1)}, u32[]{:S(2)}, u32[]{:S(2)}) collective-permute-start(bf16[256,512]{0,1:T(8,128)(2,1)S(1)} %copy.28), channel_id=1, source_target_pairs={{0,1},{1,2},{2,3},{3,4},{4,5},{5,6},{6,7},{7,8},{8,9},{9,10},{10,1... | collective-permute-start | bytes 786440 | tf_op jit(solution)/shard_map/ppermute | solution.py:42
  3.1 3.6 %collective-permute-start = (bf16[256,512]{1,0:T(8,128)(2,1)}, bf16[256,512]{1,0:T(8,128)(2,1)S(1)}, u32[]{:S(2)}, u32[]{:S(2)}) collective-permute-start(bf16[256,512]{1,0:T(8,128)(2,1)} %param.12), channel_id=1, source_target_pairs={{0,1},{1,2},{2,3},{3,4},{4,5},{5,6},{6,7},{7,8},{8,9},{9,10},{10,1... | collective-permute-start | bytes 786440 | tf_op jit(solution)/shard_map/ppermute | solution.py:42
  6.7 0.8 copy.35
  7.6 0.1 eq.59
  7.7 1.1 reduce-window.6
  8.9 0.2 slice_reduce_fusion.2
  9.1 0.1 eq.55
  9.3 0.1 fusion.33
  9.4 3.1 %collective-permute-done.3 = bf16[256,512]{0,1:T(8,128)(2,1)S(1)} collective-permute-done((bf16[256,512]{0,1:T(8,128)(2,1)S(1)}, bf16[256,512]{0,1:T(8,128)(2,1)S(1)}, u32[]{:S(2)}, u32[]{:S(2)}) %collective-permute-start.3) | collective-permute-done | bytes 262176 | tf_op jit(solution)/shard_map/ppermute | solution.py:42
  12.5 1.9 %collective-permute-start.4 = (bf16[256,512]{0,1:T(8,128)(2,1)S(1)}, bf16[256,512]{0,1:T(8,128)(2,1)}, u32[]{:S(2)}, u32[]{:S(2)}) collective-permute-start(bf16[256,512]{0,1:T(8,128)(2,1)S(1)} %collective-permute-done.3), channel_id=1, source_target_pairs={{0,1},{1,2},{2,3},{3,4},{4,5},{5,6},{6,7},{7,8},{8,9},{9,10},{10,1... | collective-permute-start | bytes 786440 | tf_op jit(solution)/shard_map/ppermute | solution.py:42
  14.4 0.9 collective-permute-done
  15.3 1.9 %collective-permute-start.1 = (bf16[256,512]{1,0:T(8,128)(2,1)S(1)}, bf16[256,512]{1,0:T(8,128)(2,1)S(1)}, u32[]{:S(2)}, u32[]{:S(2)}) collective-permute-start(bf16[256,512]{1,0:T(8,128)(2,1)S(1)} %collective-permute-done), channel_id=1, source_target_pairs={{0,1},{1,2},{2,3},{3,4},{4,5},{5,6},{6,7},{7,8},{8,9},{9,10},{10,1... | collective-permute-start | bytes 786440 | tf_op jit(solution)/shard_map/ppermute | solution.py:42
  17.2 0.1 reduce_sum.42
  17.4 6.5 %collective-permute-done.4 = bf16[256,512]{0,1:T(8,128)(2,1)} collective-permute-done((bf16[256,512]{0,1:T(8,128)(2,1)S(1)}, bf16[256,512]{0,1:T(8,128)(2,1)}, u32[]{:S(2)}, u32[]{:S(2)}) %collective-permute-start.4) | collective-permute-done | bytes 262176 | tf_op jit(solution)/shard_map/ppermute | solution.py:42
  23.9 1.9 %collective-permute-start.5 = (bf16[256,512]{0,1:T(8,128)(2,1)}, bf16[256,512]{0,1:T(8,128)(2,1)}, u32[]{:S(2)}, u32[]{:S(2)}) collective-permute-start(bf16[256,512]{0,1:T(8,128)(2,1)} %collective-permute-done.4), channel_id=1, source_target_pairs={{0,1},{1,2},{2,3},{3,4},{4,5},{5,6},{6,7},{7,8},{8,9},{9,10},{10,1... | collective-permute-start | bytes 786440 | tf_op jit(solution)/shard_map/ppermute | solution.py:42
  25.8 0.8 collective-permute-done.1
  26.6 1.9 %collective-permute-start.2 = (bf16[256,512]{1,0:T(8,128)(2,1)S(1)}, bf16[256,512]{1,0:T(8,128)(2,1)S(1)}, u32[]{:S(2)}, u32[]{:S(2)}) collective-permute-start(bf16[256,512]{1,0:T(8,128)(2,1)S(1)} %collective-permute-done.1), channel_id=1, source_target_pairs={{0,1},{1,2},{2,3},{3,4},{4,5},{5,6},{6,7},{7,8},{8,9},{9,10},{10,1... | collective-permute-start | bytes 786440 | tf_op jit(solution)/shard_map/ppermute | solution.py:42
  28.5 1.1 compare_and_fusion
  29.6 1.2 reshape.106
  30.7 0.2 slice_reduce_fusion.1
  31.0 7.2 %collective-permute-done.2 = bf16[256,512]{1,0:T(8,128)(2,1)S(1)} collective-permute-done((bf16[256,512]{1,0:T(8,128)(2,1)S(1)}, bf16[256,512]{1,0:T(8,128)(2,1)S(1)}, u32[]{:S(2)}, u32[]{:S(2)}) %collective-permute-start.2) | collective-permute-done | bytes 262176 | tf_op jit(solution)/shard_map/ppermute | solution.py:42
  38.2 1.2 pad_maximum_fusion
  39.4 0.5 copy.27
  39.9 1.2 pad_maximum_fusion.1
  41.2 7.1 %fusion.39 = (f32[4,2,256]{2,1,0:T(2,128)S(1)}, f32[4,2,256,1024]{2,3,1,0:T(8,128)}) fusion(pred[256,1024]{0,1:T(8,128)(4,1)} %compare_and_fusion, bf16[1024,4,128,1]{0,2,3,1:T(8,128)(2,1)S(1)} %bitcast.60, bf16[256,4,2,128]{3,2,1,0:T(2,128)(2,1)} %reshape.106), kind=kOutput, calls=%fused_computation.74 | convolution fusion | flops 545260544 | bytes 10231808 | tf_op jit(solution)/shard_map/sub | solution.py:75
  48.3 5.2 %fusion.7 = f32[4,128,2,256]{3,1,2,0:T(8,128)} fusion(bf16[1024,4,128,1]{0,2,3,1:T(8,128)(2,1)S(1)} %bitcast.59, f32[4,2,256,1024]{2,3,1,0:T(8,128)} %get-tuple-element.18, f32[4,2,256]{2,1,0:T(2,128)S(1)} %get-tuple-element.17), kind=kOutput, calls=%fused_computation.15 | convolution fusion | flops 541589504 | bytes 10493952 | tf_op jit(solution)/shard_map/kgts,skd->tkgd/dot_general | solution.py:77
  53.4 1.6 copy.33
  55.1 0.2 multiply_reduce_fusion.1
  55.3 0.8 convolution_convert_fusion.1
  56.2 0.3 broadcast_in_dim.12
  56.4 0.2 constant_dynamic-slice_fusion
  56.8 1.8 %collective-permute-start.8 = (bf16[1,128,1024]{2,1,0:T(8,128)(2,1)S(1)}, bf16[1,128,1024]{2,1,0:T(8,128)(2,1)S(1)}, u32[]{:S(2)}, u32[]{:S(2)}) collective-permute-start(bf16[1,128,1024]{2,1,0:T(8,128)(2,1)S(1)} %get-tuple-element.11), channel_id=1, source_target_pairs={{0,3},{1,2},{2,1},{3,0},{4,7},{5,6},{6,5},{7,4},{8,11},{9,10},{10,... | collective-permute-start | bytes 786440 | tf_op jit(solution)/shard_map/ppermute | solution.py:27
  58.6 2.6 %collective-permute-start.10 = (bf16[1,128,1024]{2,1,0:T(8,128)(2,1)S(1)}, bf16[1,128,1024]{2,1,0:T(8,128)(2,1)S(1)}, u32[]{:S(2)}, u32[]{:S(2)}) collective-permute-start(bf16[1,128,1024]{2,1,0:T(8,128)(2,1)S(1)} %get-tuple-element.9), channel_id=1, source_target_pairs={{0,5},{1,4},{2,7},{3,6},{4,1},{5,0},{6,3},{7,2},{8,13},{9,12},{10,... | collective-permute-start | bytes 786440 | tf_op jit(solution)/shard_map/ppermute | solution.py:27
  61.3 8.2 %collective-permute-done.7 = bf16[1,128,1024]{2,1,0:T(8,128)(2,1)S(1)} collective-permute-done((bf16[1,128,1024]{2,1,0:T(8,128)(2,1)S(1)}, bf16[1,128,1024]{2,1,0:T(8,128)(2,1)S(1)}, u32[]{:S(2)}, u32[]{:S(2)}) %collective-permute-start.7) | collective-permute-done | bytes 262176 | tf_op jit(solution)/shard_map/ppermute | solution.py:27
  69.5 4.5 %collective-permute-done.8 = bf16[1,128,1024]{2,1,0:T(8,128)(2,1)S(1)} collective-permute-done((bf16[1,128,1024]{2,1,0:T(8,128)(2,1)S(1)}, bf16[1,128,1024]{2,1,0:T(8,128)(2,1)S(1)}, u32[]{:S(2)}, u32[]{:S(2)}) %collective-permute-start.8) | collective-permute-done | bytes 262176 | tf_op jit(solution)/shard_map/ppermute | solution.py:27
  74.1 17.1 %collective-permute-done.9 = bf16[1,128,1024]{2,1,0:T(8,128)(2,1)S(1)} collective-permute-done((bf16[1,128,1024]{2,1,0:T(8,128)(2,1)S(1)}, bf16[1,128,1024]{2,1,0:T(8,128)(2,1)S(1)}, u32[]{:S(2)}, u32[]{:S(2)}) %collective-permute-start.9) | collective-permute-done | bytes 262176 | tf_op jit(solution)/shard_map/ppermute | solution.py:27
  91.2 4.4 %collective-permute-done.10 = bf16[1,128,1024]{2,1,0:T(8,128)(2,1)S(1)} collective-permute-done((bf16[1,128,1024]{2,1,0:T(8,128)(2,1)S(1)}, bf16[1,128,1024]{2,1,0:T(8,128)(2,1)S(1)}, u32[]{:S(2)}, u32[]{:S(2)}) %collective-permute-start.10) | collective-permute-done | bytes 262176 | tf_op jit(solution)/shard_map/ppermute | solution.py:27
  95.7 2.6 %fusion.15 = f32[1024,512]{1,0:T(8,128)} fusion(bf16[1024,1024]{1,0:T(8,128)(2,1)S(1)} %bitcast.56, bf16[1,1024,512]{2,1,0:T(8,128)(2,1)S(1)} %copy-done.11), kind=kOutput, calls=%fused_computation.21 | convolution fusion | flops 1073741824 | bytes 5242880 | tf_op jit(solution)/shard_map/dot_general | solution.py:46
  98.3 5.6 %convolution_convert_fusion = bf16[1024,1024]{1,0:T(8,128)(2,1)} fusion(f32[1024,512]{1,0:T(8,128)} %fusion.15, bf16[1,512,1024]{2,1,0:T(8,128)(2,1)S(1)} %copy-done, bf16[1024,1024]{1,0:T(8,128)(2,1)S(1)} %bitcast.57, bf16[1,1024,512]{2,1,0:T(8,128)(2,1)} %param.16), kind=kOutput, calls=%fused_computation.12 | convolution fusion | flops 2151677952 | bytes 8388608 | tf_op jit(solution)/shard_map/dot_general | solution.py:49
  103.9 13.2 %all-to-all-start = ((bf16[8,128,1024]{2,1,0:T(8,128)(2,1)}), bf16[8,128,1024]{2,1,0:T(8,128)(2,1)S(1)}, u32[]{:S(2)}, u32[]{:S(2)}) async-start(bf16[8,128,1024]{2,1,0:T(8,128)(2,1)} %bitcast.58), calls=%async_computation | async-start | bytes 4194304 | tf_op jit(solution)/shard_map/all_to_all | solution.py:105
  117.1 0.1 mul.89
  117.3 0.1 copy.34
  117.4 48.7 %all-to-all-done = bf16[8,128,1024]{2,1,0:T(8,128)(2,1)S(1)} async-done(((bf16[8,128,1024]{2,1,0:T(8,128)(2,1)}), bf16[8,128,1024]{2,1,0:T(8,128)(2,1)S(1)}, u32[]{:S(2)}, u32[]{:S(2)}) %all-to-all-start) | async-done | bytes 2097184 | tf_op jit(solution)/shard_map/all_to_all | solution.py:105
  166.2 2.8 %gather_fusion = bf16[512,1024]{1,0:T(8,128)(2,1)} fusion(bf16[1024,1024]{1,0:T(8,128)(2,1)S(1)} %bitcast.54, s32[1024]{0:T(1024)S(1)} %pad_clamp_fusion), kind=kCustom, calls=%fused_computation | custom fusion | bytes 2099200 | tf_op jit(solution)/shard_map/gather | solution.py:107
  168.9 2.4 %reshape.113 = f32[256,2,1024]{2,1,0:T(2,128)S(1)} reshape(bf16[512,1024]{1,0:T(8,128)(2,1)} %gather_fusion) | data formatting | bytes 3145728 | tf_op jit(solution)/shard_map/convert_element_type | solution.py:108
  171.3 2.6 %multiply_reduce_fusion = f32[256,1024]{1,0:T(8,128)S(1)} fusion(f32[256,2,1024]{2,1,0:T(2,128)S(1)} %reshape.113, f32[256,2]{1,0:T(8,128)S(1)} %copy.34), kind=kLoop, calls=%fused_computation.10 | loop fusion | flops 786432 | bytes 3147776 | tf_op jit(solution)/shard_map/reduce_sum | solution.py:111
  174.0 1.1 add_convert_fusion
  (50 shorter events, 0.5 us)
Async XLA Ops:
  0.0 98.3 %copy-start = (bf16[1,512,1024]{2,1,0:T(8,128)(2,1)S(1)}, bf16[1,512,1024]{2,1,0:T(8,128)(2,1)}, u32[]{:S(2)}) copy-start(bf16[1,512,1024]{2,1,0:T(8,128)(2,1)} %param.17) | copy-start | bytes 3145732
  0.0 29.6 %copy-start.5 = (bf16[256,1024]{1,0:T(8,128)(2,1)S(1)}, bf16[256,1024]{1,0:T(8,128)(2,1)}, u32[]{:S(2)}) copy-start(bf16[256,1024]{1,0:T(8,128)(2,1)} %param.10) | copy-start | bytes 1572868
  1.2 11.3 %collective-permute-start.3 = (bf16[256,512]{0,1:T(8,128)(2,1)S(1)}, bf16[256,512]{0,1:T(8,128)(2,1)S(1)}, u32[]{:S(2)}, u32[]{:S(2)}) collective-permute-start(bf16[256,512]{0,1:T(8,128)(2,1)S(1)} %copy.28), channel_id=1, source_target_pairs={{0,1},{1,2},{2,3},{3,4},{4,5},{5,6},{6,7},{7,8},{8,9},{9,10},{10,1... | collective-permute-start | bytes 786440 | tf_op jit(solution)/shard_map/ppermute | solution.py:42
  3.1 12.2 %collective-permute-start = (bf16[256,512]{1,0:T(8,128)(2,1)}, bf16[256,512]{1,0:T(8,128)(2,1)S(1)}, u32[]{:S(2)}, u32[]{:S(2)}) collective-permute-start(bf16[256,512]{1,0:T(8,128)(2,1)} %param.12), channel_id=1, source_target_pairs={{0,1},{1,2},{2,3},{3,4},{4,5},{5,6},{6,7},{7,8},{8,9},{9,10},{10,1... | collective-permute-start | bytes 786440 | tf_op jit(solution)/shard_map/ppermute | solution.py:42
  12.5 18.4 %copy-start.6 = (bf16[256,512]{0,1:T(8,128)(2,1)}, bf16[256,512]{0,1:T(8,128)(2,1)S(1)}, u32[]{:S(2)}) copy-start(bf16[256,512]{0,1:T(8,128)(2,1)S(1)} %collective-permute-done.3) | copy-start | bytes 786436
  12.5 11.4 %collective-permute-start.4 = (bf16[256,512]{0,1:T(8,128)(2,1)S(1)}, bf16[256,512]{0,1:T(8,128)(2,1)}, u32[]{:S(2)}, u32[]{:S(2)}) collective-permute-start(bf16[256,512]{0,1:T(8,128)(2,1)S(1)} %collective-permute-done.3), channel_id=1, source_target_pairs={{0,1},{1,2},{2,3},{3,4},{4,5},{5,6},{6,7},{7,8},{8,9},{9,10},{10,1... | collective-permute-start | bytes 786440 | tf_op jit(solution)/shard_map/ppermute | solution.py:42
  15.3 15.6 %copy-start.7 = (bf16[256,512]{1,0:T(8,128)(2,1)}, bf16[256,512]{1,0:T(8,128)(2,1)S(1)}, u32[]{:S(2)}) copy-start(bf16[256,512]{1,0:T(8,128)(2,1)S(1)} %collective-permute-done) | copy-start | bytes 786436
  15.3 11.3 %collective-permute-start.1 = (bf16[256,512]{1,0:T(8,128)(2,1)S(1)}, bf16[256,512]{1,0:T(8,128)(2,1)S(1)}, u32[]{:S(2)}, u32[]{:S(2)}) collective-permute-start(bf16[256,512]{1,0:T(8,128)(2,1)S(1)} %collective-permute-done), channel_id=1, source_target_pairs={{0,1},{1,2},{2,3},{3,4},{4,5},{5,6},{6,7},{7,8},{8,9},{9,10},{10,1... | collective-permute-start | bytes 786440 | tf_op jit(solution)/shard_map/ppermute | solution.py:42
  23.9 16.0 %collective-permute-start.5 = (bf16[256,512]{0,1:T(8,128)(2,1)}, bf16[256,512]{0,1:T(8,128)(2,1)}, u32[]{:S(2)}, u32[]{:S(2)}) collective-permute-start(bf16[256,512]{0,1:T(8,128)(2,1)} %collective-permute-done.4), channel_id=1, source_target_pairs={{0,1},{1,2},{2,3},{3,4},{4,5},{5,6},{6,7},{7,8},{8,9},{9,10},{10,1... | collective-permute-start | bytes 786440 | tf_op jit(solution)/shard_map/ppermute | solution.py:42
  26.6 4.4 %copy-start.8 = (bf16[256,512]{1,0:T(8,128)(2,1)}, bf16[256,512]{1,0:T(8,128)(2,1)S(1)}, u32[]{:S(2)}) copy-start(bf16[256,512]{1,0:T(8,128)(2,1)S(1)} %collective-permute-done.1) | copy-start | bytes 786436
  26.6 11.6 %collective-permute-start.2 = (bf16[256,512]{1,0:T(8,128)(2,1)S(1)}, bf16[256,512]{1,0:T(8,128)(2,1)S(1)}, u32[]{:S(2)}, u32[]{:S(2)}) collective-permute-start(bf16[256,512]{1,0:T(8,128)(2,1)S(1)} %collective-permute-done.1), channel_id=1, source_target_pairs={{0,1},{1,2},{2,3},{3,4},{4,5},{5,6},{6,7},{7,8},{8,9},{9,10},{10,1... | collective-permute-start | bytes 786440 | tf_op jit(solution)/shard_map/ppermute | solution.py:42
  53.4 1.6 copy-start.3
  53.4 1.9 %copy-start.9 = (f32[1024]{0:T(1024)S(1)}, f32[1024]{0:T(1024)}, u32[]{:S(2)}) copy-start(f32[1024]{0:T(1024)} %param.14) | copy-start | bytes 12292
  55.1 1.1 copy-start.1
  56.7 39.0 %copy-start.11 = (bf16[1,1024,512]{2,1,0:T(8,128)(2,1)S(1)}, bf16[1,1024,512]{2,1,0:T(8,128)(2,1)}, u32[]{:S(2)}) copy-start(bf16[1,1024,512]{2,1,0:T(8,128)(2,1)} %param.15) | copy-start | bytes 3145732
  56.7 4.5 %collective-permute-start.6 = (bf16[1,128,1024]{2,1,0:T(8,128)(2,1)S(1)}, bf16[1,128,1024]{2,1,0:T(8,128)(2,1)S(1)}, u32[]{:S(2)}, u32[]{:S(2)}) collective-permute-start(bf16[1,128,1024]{2,1,0:T(8,128)(2,1)S(1)} %get-tuple-element.13), channel_id=1, source_target_pairs={{0,1},{1,0},{2,3},{3,2},{4,5},{5,4},{6,7},{7,6},{8,9},{9,8},{10,11... | collective-permute-start | bytes 786440 | tf_op jit(solution)/shard_map/ppermute | solution.py:27
  56.8 12.8 %collective-permute-start.7 = (bf16[1,128,1024]{2,1,0:T(8,128)(2,1)S(1)}, bf16[1,128,1024]{2,1,0:T(8,128)(2,1)S(1)}, u32[]{:S(2)}, u32[]{:S(2)}) collective-permute-start(bf16[1,128,1024]{2,1,0:T(8,128)(2,1)S(1)} %get-tuple-element.12), channel_id=1, source_target_pairs={{0,2},{1,3},{2,0},{3,1},{4,6},{5,7},{6,4},{7,5},{8,10},{9,11},{10,... | collective-permute-start | bytes 786440 | tf_op jit(solution)/shard_map/ppermute | solution.py:27
  56.8 17.2 %collective-permute-start.8 = (bf16[1,128,1024]{2,1,0:T(8,128)(2,1)S(1)}, bf16[1,128,1024]{2,1,0:T(8,128)(2,1)S(1)}, u32[]{:S(2)}, u32[]{:S(2)}) collective-permute-start(bf16[1,128,1024]{2,1,0:T(8,128)(2,1)S(1)} %get-tuple-element.11), channel_id=1, source_target_pairs={{0,3},{1,2},{2,1},{3,0},{4,7},{5,6},{6,5},{7,4},{8,11},{9,10},{10,... | collective-permute-start | bytes 786440 | tf_op jit(solution)/shard_map/ppermute | solution.py:27
  58.6 32.6 %collective-permute-start.9 = (bf16[1,128,1024]{2,1,0:T(8,128)(2,1)S(1)}, bf16[1,128,1024]{2,1,0:T(8,128)(2,1)S(1)}, u32[]{:S(2)}, u32[]{:S(2)}) collective-permute-start(bf16[1,128,1024]{2,1,0:T(8,128)(2,1)S(1)} %get-tuple-element.10), channel_id=1, source_target_pairs={{0,4},{1,5},{2,6},{3,7},{4,0},{5,1},{6,2},{7,3},{8,12},{9,13},{10,... | collective-permute-start | bytes 786440 | tf_op jit(solution)/shard_map/ppermute | solution.py:27
  58.6 37.0 %collective-permute-start.10 = (bf16[1,128,1024]{2,1,0:T(8,128)(2,1)S(1)}, bf16[1,128,1024]{2,1,0:T(8,128)(2,1)S(1)}, u32[]{:S(2)}, u32[]{:S(2)}) collective-permute-start(bf16[1,128,1024]{2,1,0:T(8,128)(2,1)S(1)} %get-tuple-element.9), channel_id=1, source_target_pairs={{0,5},{1,4},{2,7},{3,6},{4,1},{5,0},{6,3},{7,2},{8,13},{9,12},{10,... | collective-permute-start | bytes 786440 | tf_op jit(solution)/shard_map/ppermute | solution.py:27
  61.2 34.4 %collective-permute-start.11 = (bf16[1,128,1024]{2,1,0:T(8,128)(2,1)S(1)}, bf16[1,128,1024]{2,1,0:T(8,128)(2,1)S(1)}, u32[]{:S(2)}, u32[]{:S(2)}) collective-permute-start(bf16[1,128,1024]{2,1,0:T(8,128)(2,1)S(1)} %get-tuple-element.8), channel_id=1, source_target_pairs={{0,6},{1,7},{2,4},{3,5},{4,2},{5,3},{6,0},{7,1},{8,14},{9,15},{10,... | collective-permute-start | bytes 786440 | tf_op jit(solution)/shard_map/ppermute | solution.py:27
  69.5 26.2 %collective-permute-start.12 = (bf16[1,128,1024]{2,1,0:T(8,128)(2,1)S(1)}, bf16[1,128,1024]{2,1,0:T(8,128)(2,1)S(1)}, u32[]{:S(2)}, u32[]{:S(2)}) collective-permute-start(bf16[1,128,1024]{2,1,0:T(8,128)(2,1)S(1)} %get-tuple-element.7), channel_id=1, source_target_pairs={{0,7},{1,6},{2,5},{3,4},{4,3},{5,2},{6,1},{7,0},{8,15},{9,14},{10,... | collective-permute-start | bytes 786440 | tf_op jit(solution)/shard_map/ppermute | solution.py:27
  103.9 13.3 %copy-start.10 = (f32[256,2]{0,1:T(2,128)S(1)}, f32[256,2]{0,1:T(2,128)}, u32[]{:S(2)}) copy-start(f32[256,2]{0,1:T(2,128)} %param.19) | copy-start | bytes 6148
  103.9 62.2 %all-to-all-start = ((bf16[8,128,1024]{2,1,0:T(8,128)(2,1)}), bf16[8,128,1024]{2,1,0:T(8,128)(2,1)S(1)}, u32[]{:S(2)}, u32[]{:S(2)}) async-start(bf16[8,128,1024]{2,1,0:T(8,128)(2,1)} %bitcast.58), calls=%async_computation | async-start | bytes 4194304 | tf_op jit(solution)/shard_map/all_to_all | solution.py:105
  171.3 2.7 %copy-start.2 = (f32[256,1024]{1,0:T(8,128)S(1)}, f32[256,1024]{1,0:T(8,128)}, u32[]{:S(2)}) copy-start(f32[256,1024]{1,0:T(8,128)} %copy-done.1) | copy-start | bytes 3145732
  171.3 2.7 %copy-start.4 = (bf16[256,1024]{1,0:T(8,128)(2,1)S(1)}, bf16[256,1024]{1,0:T(8,128)(2,1)}, u32[]{:S(2)}) copy-start(bf16[256,1024]{1,0:T(8,128)(2,1)} %param.13) | copy-start | bytes 1572868
